TPU v7x, 32 devices: a whole 2x2x4 slice. The times are simulated.
32 devices in a mesh: mem: 4 (over y, x), cell: 8 (over z, core).
Axes of the slice: x: 2, y: 2, z: 4, core: 2. Of those that a mesh axis runs over, the one named last changes fastest.
Arguments:
- depth: float32 [64, 131072], P('mem', 'cell'), may hold values from 1 to 3
- discharge: float32 [64, 131072], P('mem', 'cell'), may hold values from -1.5 to 1.5
- gate: int32 [131072], P('cell'), may hold values from 0 to 1, as said below
- pump: int32 [2, 131072], P(None, 'cell'), may hold values 0 or 1
- pump_rate: float32 [131072], P('cell'), may hold values from 1 to 5
- obs_index: int32 [8, 512], P('cell'), may hold values from 0 to 16383, as said below
- obs_value: float32 [8, 512], P('cell'), may hold values from 1 to 3
- obs_error: float32 [8, 512], P('cell'), may hold values from 0.25 to 1.04
Outputs:
- depth_analysis: float32 [64, 131072], P('mem', 'cell')
- discharge_analysis: float32 [64, 131072], P('mem', 'cell')
Inputs may be any that keep to these rules, and one draw needn't show every extreme that they name: The gate on the first face of every slab after the first (cells s * 16384 with s >= 1) is open. `obs_index`: the offsets of one slab are distinct.
All inputs are finite; a program needn't handle non-finite values. No bound on the sum of `pump` on one device may be relied on, other than what follows from the above.
Results may differ from a plain program's by a relative error of at most 0.0003.
Values sent between devices are 32-bit elements; how exact they have to be, the bound alone decides.
A program may use at most 64 MiB of HBM per device.

v0:
```python
import jax
import jax.numpy as jnp
from jax import lax
from jax.sharding import PartitionSpec as P

PER = 512
NS_ITERS = 12
gravity = 9.81
step_dt = 0.06


def padded_2(block, sides, width):
    for axis, dim in sides:
        count = lax.axis_size(axis)
        forward = [(i, i + 1) for i in range(count - 1)]
        backward = [(target, source) for source, target in forward]
        low = lax.ppermute(
            lax.slice_in_dim(block, block.shape[dim] - width, None, axis=dim), axis, forward
        )
        high = lax.ppermute(lax.slice_in_dim(block, 0, width, axis=dim), axis, backward)
        block = jnp.concatenate([low, block, high], axis=dim)
    return block


def face_fluxes(depth_left, flow_left, depth_right, flow_right, faces):
    opened = faces > 0.5
    safe_dl = jnp.where(opened, depth_left, 1.0)
    safe_fl = jnp.where(opened, flow_left, 0.0)
    safe_dr = jnp.where(opened, depth_right, 1.0)
    safe_fr = jnp.where(opened, flow_right, 0.0)
    speed_left = safe_fl / safe_dl
    speed_right = safe_fr / safe_dr
    wave_left = jnp.sqrt(gravity * safe_dl)
    wave_right = jnp.sqrt(gravity * safe_dr)
    slowest = jnp.minimum(jnp.minimum(speed_left - wave_left, speed_right - wave_right), 0.0)
    fastest = jnp.maximum(jnp.maximum(speed_left + wave_left, speed_right + wave_right), 0.0)
    moment_left = safe_fl * speed_left + 0.5 * gravity * safe_dl * safe_dl
    moment_right = safe_fr * speed_right + 0.5 * gravity * safe_dr * safe_dr
    spread = fastest - slowest
    mass = (
        fastest * safe_fl - slowest * safe_fr + slowest * fastest * (safe_dr - safe_dl)
    ) / spread
    moment = (
        fastest * moment_left - slowest * moment_right + slowest * fastest * (safe_fr - safe_fl)
    ) / spread
    mass = jnp.where(opened, mass, 0.0)
    left_side = jnp.where(opened, moment, 0.5 * gravity * depth_left * depth_left)
    right_side = jnp.where(opened, moment, 0.5 * gravity * depth_right * depth_right)
    return (mass, left_side, right_side)


def advance(depth_pad, flow_pad, faces, inflow):
    mass, left_side, right_side = face_fluxes(
        depth_pad[..., :-1], flow_pad[..., :-1], depth_pad[..., 1:], flow_pad[..., 1:], faces
    )
    depth_new = depth_pad[..., 1:-1] - step_dt * (mass[..., 1:] - mass[..., :-1]) + step_dt * inflow
    flow_new = flow_pad[..., 1:-1] - step_dt * (left_side[..., 1:] - right_side[..., :-1])
    return (depth_new, flow_new)


def batch_product(first, second):
    return jnp.einsum("uij,ujk->uik", first, second, precision=lax.Precision.HIGHEST)


def transform_units(grams, cross, factor_rho):
    count = grams.shape[-1]
    identity = jnp.eye(count, dtype=jnp.float32)
    system = identity + factor_rho * factor_rho / (count - 1) * grams
    norm_scale = jnp.sqrt(jnp.sum(system * system, axis=(1, 2)))
    iterate = system / norm_scale[:, None, None]
    inverse = jnp.broadcast_to(identity, system.shape)

    def newton_step(turn, carry):
        current, invroot = carry
        factor = 1.5 * identity - 0.5 * batch_product(invroot, current)
        return (batch_product(current, factor), batch_product(factor, invroot))

    iterate, inverse = lax.fori_loop(0, NS_ITERS, newton_step, (iterate, inverse))
    root_weight = inverse / jnp.sqrt(norm_scale)[:, None, None]
    solved = batch_product(inverse, inverse) / norm_scale[:, None, None]
    mean_weight = (
        factor_rho
        / (count - 1)
        * jnp.einsum("uij,uj->ui", solved, cross, precision=lax.Precision.HIGHEST)
    )
    return factor_rho * (root_weight + mean_weight[:, :, None])


def window_sums(block_grams, block_cross):
    grams = block_grams[:-2] + block_grams[1:-1] + block_grams[2:]
    cross = block_cross[:-2] + block_cross[1:-1] + block_cross[2:]
    return (grams, cross)


def shards(depth, discharge, gate, pump, pump_rate, obs_index, obs_value, obs_error):
    member_rows = depth.shape[0]
    cell_count = depth.shape[1]
    slab_count = lax.axis_size("cell")
    quarter_count = lax.axis_size("mem")
    members = member_rows * quarter_count
    quart_cells = cell_count // quarter_count
    sub_count = quart_cells // PER
    obs_count = obs_index.shape[1]
    total_obs = obs_count * slab_count
    slab_here = lax.axis_index("cell")
    first_slab = slab_here == 0
    last_slab = slab_here == slab_count - 1
    left_open = gate.at[0].set(jnp.where(first_slab, 0, gate[0]))
    right_face = jnp.where(last_slab, 0, 1).astype(jnp.int32).reshape(1)
    faces = jnp.concatenate([left_open, right_face]).astype(jnp.float32)
    depth_now, flow_now = (depth, discharge)
    for step in range(pump.shape[0]):
        padded = padded_2(jnp.stack([depth_now, flow_now]), (("cell", 2),), 1)
        inflow = pump_rate * pump[step].astype(jnp.float32)
        depth_now, flow_now = advance(padded[0], padded[1], faces, inflow)
    offsets = obs_index[0]
    precision_obs = 1.0 / obs_error[0]
    values_obs = obs_value[0]
    value_row = jnp.zeros((cell_count,), jnp.float32).at[offsets].set(values_obs)
    prec_row = jnp.zeros((cell_count,), jnp.float32).at[offsets].set(precision_obs)
    stacked = jnp.concatenate([depth_now, value_row[None, :], prec_row[None, :]], axis=0)
    extended = padded_2(stacked, (("cell", 1),), PER)
    row_total = extended.shape[0]
    seen_local = depth_now[:, offsets]
    seen_all = lax.all_gather(seen_local, "mem", axis=0, tiled=True)
    seen_mean = jnp.mean(seen_all, axis=0)
    scaled_seen = (seen_all - seen_mean[None, :]) * precision_obs[None, :]
    innov_seen = (values_obs - seen_mean) * precision_obs
    total_misfit, total_spread = lax.psum(
        (jnp.sum(innov_seen * innov_seen), jnp.sum(scaled_seen * scaled_seen) / (members - 1)),
        "cell",
    )
    head = extended[:, :cell_count].reshape(row_total, quarter_count, quart_cells)[:, :, :PER]
    core = extended[:, PER : PER + cell_count].reshape(row_total, quarter_count, quart_cells)
    tail = extended[:, 2 * PER :].reshape(row_total, quarter_count, quart_cells)[
        :, :, quart_cells - PER :
    ]
    windows = jnp.concatenate([head, core, tail], axis=2)
    flow_quarters = flow_now.reshape(member_rows, quarter_count, quart_cells)
    moved_depth, moved_flow = (
        lax.all_to_all(windows[:member_rows], "mem", split_axis=1, concat_axis=0, tiled=True),
        lax.all_to_all(flow_quarters, "mem", split_axis=1, concat_axis=0, tiled=True),
    )
    window_depth = moved_depth[:, 0]
    quarter_flow = moved_flow[:, 0]
    obs_window = lax.dynamic_index_in_dim(
        windows[member_rows:], lax.axis_index("mem"), 1, keepdims=False
    )
    window_mean = jnp.mean(window_depth, axis=0)
    scaled = (window_depth - window_mean[None, :]) * obs_window[1][None, :]
    innov = (obs_window[0] - window_mean) * obs_window[1]
    blocks = scaled.reshape(members, sub_count + 2, PER)
    block_grams = jnp.einsum("ibr,jbr->bij", blocks, blocks, precision=lax.Precision.HIGHEST)
    block_cross = jnp.einsum(
        "ibr,br->bi", blocks, innov.reshape(sub_count + 2, PER), precision=lax.Precision.HIGHEST
    )
    grams, cross = window_sums(block_grams, block_cross)
    factor_rho = jnp.sqrt(total_misfit / (total_spread + total_obs))
    mixing = transform_units(grams, cross, factor_rho)
    fields = jnp.stack([window_depth[:, PER : PER + quart_cells], quarter_flow]).reshape(
        2, members, sub_count, PER
    )
    field_mean = jnp.mean(fields, axis=1, keepdims=True)
    analysed = field_mean + jnp.einsum(
        "fipr,pij->fjpr", fields - field_mean, mixing, precision=lax.Precision.HIGHEST
    )
    restored = lax.all_to_all(
        analysed.reshape(2, members, quart_cells), "mem", split_axis=1, concat_axis=2, tiled=True
    )
    return (restored[0], restored[1])


def solution(mesh):
    return jax.shard_map(
        shards,
        mesh=mesh,
        in_specs=(
            P("mem", "cell"),
            P("mem", "cell"),
            P("cell"),
            P(None, "cell"),
            P("cell"),
            P("cell", None),
            P("cell", None),
            P("cell", None),
        ),
        out_specs=(P("mem", "cell"), P("mem", "cell")),
        check_vma=False,
    )
```

profile of v0, /device:TPU:0, one launch (start us, length us, event | category | flops | bytes accessed | tf_op | source)
XLA Modules:
  0.0 180.7 jit_solution(2937933916349297083)
XLA Ops:
  3.7 3.0 %collective-permute-start = (f32[2,16,1]{2,1,0:T(8,128)S(1)}, f32[2,16,1]{2,1,0:T(8,128)S(1)}, u32[]{:S(2)}, u32[]{:S(2)}) collective-permute-start(f32[2,16,1]{2,1,0:T(8,128)S(1)} %get-tuple-element.88), channel_id=1, source_target_pairs={{0,1},{1,2},{2,3},{3,4},{4,5},{5,6},{6,7},{8,9},{9,10},{10,11},{11... | collective-permute-start | bytes 392 | tf_op jit(solution)/shard_map/ppermute | solution.py:17
  7.4 1.5 pad_maximum_fusion
  10.4 2.5 %scatter_custom_fusion.1 = f32[16384]{0:T(1024)S(1)} fusion(s32[512]{0:T(512)S(1)} %bitcast.152, f32[512]{0:T(512)S(1)} %bitcast.146, f32[]{:T(128)} %constant.71.clone.1), kind=kCustom, calls=%fused_computation.138 | custom fusion | bytes 65540 | tf_op jit(solution)/shard_map/scatter | solution.py:120
  12.9 2.5 %scatter_custom_fusion = f32[16384]{0:T(1024)S(1)} fusion(s32[512]{0:T(512)S(1)} %bitcast.153, f32[512]{0:T(512)S(1)} %bitcast.154, f32[]{:T(128)} %constant.71.clone.1), kind=kCustom, calls=%fused_computation.140 | custom fusion | bytes 65540 | tf_op jit(solution)/shard_map/scatter | solution.py:119
  15.4 3.1 %concatenate.34 = f32[2,16,16386]{2,1,0:T(8,128)S(1)} concatenate(f32[2,16,1]{2,1,0:T(8,128)S(1)} %collective-permute-done, f32[2,16,16384]{2,1,0:T(8,128)} %pad_maximum_fusion, f32[2,16,1]{2,1,0:T(8,128)S(1)} %collective-permute-done.1), dimensions={2} | concatenate | bytes 4194816 | tf_op jit(solution)/shard_map/concatenate | solution.py:21
  18.6 2.2 %fusion.12 = (f32[16,16385]{1,0:T(8,128)S(1)}, f32[16,16385]{1,0:T(8,128)S(1)}, f32[16,16385]{1,0:T(8,128)S(1)}, f32[16,16385]{1,0:T(8,128)S(1)}) fusion(f32[16,16386]{1,0:T(8,128)S(1)} %get-tuple-element.82, pred[16385]{0:T(1024)(128)(4,1)S(1)} %fusion.58, f32[16,16386]{1,0:T(8,128)S(1)} %get-tuple-element.81), kind=kLoop, calls=%fused_computation.43 | loop fusion | flops 10748560 | bytes 8405505 | tf_op jit(solution)/shard_map/div | solution.py:43
  20.8 1.4 fusion.26
  23.6 5.2 %collective-permute-start.2 = (f32[2,16,1]{2,1,0:T(8,128)S(1)}, f32[2,16,1]{2,1,0:T(8,128)S(1)}, u32[]{:S(2)}, u32[]{:S(2)}) collective-permute-start(f32[2,16,1]{2,1,0:T(8,128)S(1)} %get-tuple-element.86), channel_id=1, source_target_pairs={{0,1},{1,2},{2,3},{3,4},{4,5},{5,6},{6,7},{8,9},{9,10},{10,11},{11... | collective-permute-start | bytes 392 | tf_op jit(solution)/shard_map/ppermute | solution.py:17
  28.8 1.5 pad_maximum_fusion.1
  30.3 3.1 %concatenate.36 = f32[2,16,16386]{2,1,0:T(8,128)S(1)} concatenate(f32[2,16,1]{2,1,0:T(8,128)S(1)} %collective-permute-done.2, f32[2,16,16384]{2,1,0:T(8,128)} %pad_maximum_fusion.1, f32[2,16,1]{2,1,0:T(8,128)S(1)} %collective-permute-done.3), dimensions={2} | concatenate | bytes 4194816 | tf_op jit(solution)/shard_map/concatenate | solution.py:21
  33.5 2.2 %fusion.19 = (f32[16,16385]{1,0:T(8,128)S(1)}, f32[16,16385]{1,0:T(8,128)S(1)}, f32[16,16385]{1,0:T(8,128)S(1)}, f32[16,16385]{1,0:T(8,128)S(1)}) fusion(f32[16,16386]{1,0:T(8,128)S(1)} %get-tuple-element.80, pred[16385]{0:T(1024)(128)(4,1)S(1)} %fusion.58, f32[16,16386]{1,0:T(8,128)S(1)} %get-tuple-element.79), kind=kLoop, calls=%fused_computation.50 | loop fusion | flops 10748560 | bytes 8405505 | tf_op jit(solution)/shard_map/div | solution.py:43
  36.3 3.6 %collective-permute-start.4 = (f32[18,512]{1,0:T(8,128)S(1)}, f32[18,512]{1,0:T(8,128)S(1)}, u32[]{:S(2)}, u32[]{:S(2)}) collective-permute-start(f32[18,512]{1,0:T(8,128)S(1)} %get-tuple-element.91), channel_id=1, source_target_pairs={{0,1},{1,2},{2,3},{3,4},{4,5},{5,6},{6,7},{8,9},{9,10},{10,11},{11... | collective-permute-start | bytes 110600 | tf_op jit(solution)/shard_map/ppermute | solution.py:17
  42.2 4.6 %copy.124 = f32[16,16384]{0,1:T(8,128)} copy(f32[16,16384]{1,0:T(8,128)S(1)} %fusion.35) | data formatting | bytes 2097152 | tf_op jit(solution)/shard_map/add | solution.py:56
  47.8 4.5 %all-to-all-start.1 = ((f32[16,4,4096]{2,0,1:T(8,128)}), f32[16,4,4096]{2,0,1:T(8,128)}, u32[]{:S(2)}, u32[]{:S(2)}) async-start(f32[16,4,4096]{2,0,1:T(8,128)} %bitcast.97), calls=%async_computation.1 | async-start | bytes 2097152 | tf_op jit(solution)/shard_map/all_to_all | solution.py:142
  52.4 4.4 %gather_fusion = f32[512,16]{1,0:T(8,128)S(1)} fusion(f32[16,16384]{0,1:T(8,128)} %copy.124, s32[1024]{0:T(1024)S(1)} %pad_clamp_fusion), kind=kCustom, calls=%fused_computation | custom fusion | bytes 67584 | tf_op jit(solution)/shard_map/gather | solution.py:124
  56.9 12.8 %all-gather = f32[64,512]{1,0:T(8,128)S(1)} all-gather(f32[16,512]{1,0:T(8,128)S(1)} %copy.125), channel_id=2, replica_groups=mesh['mem'=4,'cell'=8] {'mem'}, dimensions={0}, use_global_device_ids=true | all-gather | bytes 163840 | tf_op jit(solution)/shard_map/all_gather | solution.py:125
  69.8 1.8 %pad_maximum_fusion.6 = (f32[18,16384]{1,0:T(8,128)}, f32[18,16384]{1,0:T(8,128)}) fusion(f32[18,512]{1,0:T(8,128)S(1)} %collective-permute-done.4, f32[1,16384]{1,0:T(1,128)S(1)} %bitcast.133, f32[1,16384]{1,0:T(1,128)S(1)} %bitcast.137, f32[16,16384]{1,0:T(8,128)S(1)} %fusion.35, f32[18,512]{1,0:T(8,128)S(1)} %collective-permute-done.5), kind=kLoop, calls=%fused_computation.31 | loop fusion | flops 1769472 | bytes 3612672 | tf_op jit(solution)/shard_map/concatenate | solution.py:21
  71.6 3.1 %reshape.149 = f32[18,4,4096]{2,1,0:T(4,128)} reshape(f32[18,16384]{1,0:T(8,128)} %get-tuple-element.89) | data formatting | bytes 2359296 | tf_op jit(solution)/shard_map/reshape | solution.py:133
  75.7 1.8 %reshape.150 = f32[18,4,4096]{2,1,0:T(4,128)} reshape(f32[18,16384]{1,0:T(8,128)S(1)} %copy-done) | data formatting | bytes 2359296 | tf_op jit(solution)/shard_map/reshape | solution.py:135
  79.9 3.7 %all-to-all-start = ((f32[16,4,5120]{2,0,1:T(8,128)}), f32[16,4,5120]{2,0,1:T(8,128)S(1)}, u32[]{:S(2)}, u32[]{:S(2)}) async-start(f32[16,4,5120]{2,0,1:T(8,128)} %slice.254), calls=%async_computation | async-start | bytes 2621440 | tf_op jit(solution)/shard_map/all_to_all | solution.py:141
  85.4 16.1 %all-reduce = (f32[]{:T(128)}, f32[]{:T(128)}) all-reduce(f32[]{:T(128)} %get-tuple-element.104, f32[]{:T(128)S(6)} %div.103), channel_id=1, replica_groups=mesh['mem'=4,'cell'=8] {'cell'}, use_global_device_ids=true, to_apply=%region_5.6 | all-reduce | flops 2 | bytes 16 | tf_op jit(solution)/shard_map/psum | solution.py:129
  103.5 2.8 %copy.150 = f32[8,8,8,512]{3,2,1,0:T(8,128)} copy(f32[8,8,8,512]{3,1,2,0:T(8,128)} %bitcast.55) | data formatting | bytes 2097152
  109.3 1.7 squeeze.49
  111.0 1.9 %subtract_multiply_fusion = f32[64,10,512]{2,1,0:T(8,128)S(1)} fusion(f32[64,10,512]{2,1,0:T(8,128)} %squeeze.49, f32[10,512]{1,0:T(8,128)S(1)} %mul.260, f32[10,512]{1,0:T(8,128)S(1)} %div.108), kind=kLoop, calls=%fused_computation.22 | loop fusion | flops 655360 | bytes 2662400 | tf_op jit(solution)/shard_map/mul | solution.py:150
  112.9 2.8 %fusion.43 = f32[10,64,64]{2,1,0:T(8,128)S(1)} fusion(f32[64,10,512]{2,1,0:T(8,128)S(1)} %subtract_multiply_fusion), kind=kOutput, calls=%fused_computation.98 | convolution fusion | flops 251658240 | bytes 1474560 | tf_op jit(solution)/shard_map/ibr,jbr->bij/dot_general | solution.py:153
  115.7 2.0 %fusion.41 = f32[10,1,64]{2,1,0:T(1,128)S(1)} fusion(f32[64,10,512]{2,1,0:T(8,128)S(1)} %subtract_multiply_fusion, f32[10,512,1]{1,0,2:T(8,128)S(1)} %multiply_bitcast_fusion), kind=kOutput, calls=%fused_computation.96 | convolution fusion | flops 3932160 | bytes 1333760 | tf_op jit(solution)/shard_map/ibr,br->bi/dot_general | solution.py:154
  118.1 19.9 %while.14 = (s32[]{:T(128)}, f32[8,64,64]{1,2,0:T(8,128)S(1)}, f32[8,64,64]{2,1,0:T(8,128)S(1)}, s32[]{:T(128)}) while((s32[]{:T(128)}, f32[8,64,64]{1,2,0:T(8,128)S(1)}, f32[8,64,64]{2,1,0:T(8,128)S(1)}, s32[]{:T(128)}) %tuple.56), condition=%wide.region_11.12_spmd.clone, body=%wide.region_10.11_spmd.clone.sunk | while | flops 75571200 | bytes 1736757 | solution.py:78
  138.9 2.1 %bitcast_add_fusion = f32[2,64,8,512]{3,1,0,2:T(8,128)S(1)} fusion(f32[2,64,8,512]{3,1,0,2:T(8,128)S(1)} %copy_dynamic-update-slice_fusion, f32[2,8,512]{2,0,1:T(2,128)S(1)} %broadcast_multiply_fusion, f32[8,64,64]{2,1,0:T(8,128)S(1)} %get-tuple-element.36, f32[8,64]{1,0:T(8,128)S(1)} %broadcast_multiply_fusion.2, f32[8]{0:T(128)S(1)} %get-tuple-element.105, ...), kind=kOutput, calls=%fused_computation.19 | convolution fusion | flops 403800064 | bytes 4360228 | tf_op jit(solution)/shard_map/fipr,pij->fjpr/dot_general | solution.py:164
  142.3 2.8 %reshape.183 = f32[2,64,4096]{2,0,1:T(2,128)} reshape(f32[2,64,8,512]{3,2,0,1:T(8,128)S(1)} %copy.145) | data formatting | bytes 4194304 | tf_op jit(solution)/shard_map/reshape | solution.py:168
  145.1 29.7 %all_to_all.45 = f32[2,64,4096]{2,0,1:T(2,128)S(1)} all-to-all(f32[2,64,4096]{2,0,1:T(2,128)} %reshape.183), channel_id=1, replica_groups=mesh['mem'=4,'cell'=8] {'mem'}, dimensions={1} | all-to-all | bytes 4194304 | tf_op jit(solution)/shard_map/all_to_all | solution.py:167
  176.9 1.6 copy.152
  179.1 1.6 copy.151
  (172 shorter events, 42.7 us)
Async XLA Ops:
  1.5 5.9 %copy-start.2 = (f32[16,16384]{1,0:T(8,128)S(1)}, f32[16,16384]{1,0:T(8,128)}, u32[]{:S(2)}) copy-start(f32[16,16384]{1,0:T(8,128)} %param.12) | copy-start | bytes 3145732
  1.5 5.9 %copy-start.3 = (f32[16,16384]{1,0:T(8,128)S(1)}, f32[16,16384]{1,0:T(8,128)}, u32[]{:S(2)}) copy-start(f32[16,16384]{1,0:T(8,128)} %param.13) | copy-start | bytes 3145732
  2.5 13.0 %collective-permute-start.1 = (f32[2,16,1]{2,1,0:T(8,128)S(1)}, f32[2,16,1]{2,1,0:T(8,128)S(1)}, u32[]{:S(2)}, u32[]{:S(2)}) collective-permute-start(f32[2,16,1]{2,1,0:T(8,128)S(1)} %get-tuple-element.87), channel_id=1, source_target_pairs={{1,0},{2,1},{3,2},{4,3},{5,4},{6,5},{7,6},{9,8},{10,9},{11,10},{12... | collective-permute-start | bytes 392 | tf_op jit(solution)/shard_map/ppermute | solution.py:20
  3.7 11.7 %collective-permute-start = (f32[2,16,1]{2,1,0:T(8,128)S(1)}, f32[2,16,1]{2,1,0:T(8,128)S(1)}, u32[]{:S(2)}, u32[]{:S(2)}) collective-permute-start(f32[2,16,1]{2,1,0:T(8,128)S(1)} %get-tuple-element.88), channel_id=1, source_target_pairs={{0,1},{1,2},{2,3},{3,4},{4,5},{5,6},{6,7},{8,9},{9,10},{10,11},{11... | collective-permute-start | bytes 392 | tf_op jit(solution)/shard_map/ppermute | solution.py:17
  7.4 1.5 copy-start.13
  7.4 1.5 copy-start.14
  7.4 2.8 %copy-start.9 = (s32[2,16384]{1,0:T(2,128)S(1)}, s32[2,16384]{1,0:T(2,128)}, u32[]{:S(2)}) copy-start(s32[2,16384]{1,0:T(2,128)} %param.15) | copy-start | bytes 393220
  7.4 5.4 %copy-start.11 = (f32[16384]{0:T(1024)S(1)}, f32[16384]{0:T(1024)}, u32[]{:S(2)}) copy-start(f32[16384]{0:T(1024)} %param.16) | copy-start | bytes 196612
  7.4 5.5 %copy-start.12 = (f32[1,512]{1,0:T(1,128)S(1)}, f32[1,512]{1,0:T(1,128)}, u32[]{:S(2)}) copy-start(f32[1,512]{1,0:T(1,128)} %param.18) | copy-start | bytes 6148
  22.3 8.0 %collective-permute-start.3 = (f32[2,16,1]{2,1,0:T(8,128)S(1)}, f32[2,16,1]{2,1,0:T(8,128)S(1)}, u32[]{:S(2)}, u32[]{:S(2)}) collective-permute-start(f32[2,16,1]{2,1,0:T(8,128)S(1)} %get-tuple-element.85), channel_id=1, source_target_pairs={{1,0},{2,1},{3,2},{4,3},{5,4},{6,5},{7,6},{9,8},{10,9},{11,10},{12... | collective-permute-start | bytes 392 | tf_op jit(solution)/shard_map/ppermute | solution.py:20
  23.6 6.7 %collective-permute-start.2 = (f32[2,16,1]{2,1,0:T(8,128)S(1)}, f32[2,16,1]{2,1,0:T(8,128)S(1)}, u32[]{:S(2)}, u32[]{:S(2)}) collective-permute-start(f32[2,16,1]{2,1,0:T(8,128)S(1)} %get-tuple-element.86), channel_id=1, source_target_pairs={{0,1},{1,2},{2,3},{3,4},{4,5},{5,6},{6,7},{8,9},{9,10},{10,11},{11... | collective-permute-start | bytes 392 | tf_op jit(solution)/shard_map/ppermute | solution.py:17
  36.3 33.4 %collective-permute-start.4 = (f32[18,512]{1,0:T(8,128)S(1)}, f32[18,512]{1,0:T(8,128)S(1)}, u32[]{:S(2)}, u32[]{:S(2)}) collective-permute-start(f32[18,512]{1,0:T(8,128)S(1)} %get-tuple-element.91), channel_id=1, source_target_pairs={{0,1},{1,2},{2,3},{3,4},{4,5},{5,6},{6,7},{8,9},{9,10},{10,11},{11... | collective-permute-start | bytes 110600 | tf_op jit(solution)/shard_map/ppermute | solution.py:17
  40.0 29.8 %collective-permute-start.5 = (f32[18,512]{1,0:T(8,128)S(1)}, f32[18,512]{1,0:T(8,128)S(1)}, u32[]{:S(2)}, u32[]{:S(2)}) collective-permute-start(f32[18,512]{1,0:T(8,128)S(1)} %get-tuple-element.92), channel_id=1, source_target_pairs={{1,0},{2,1},{3,2},{4,3},{5,4},{6,5},{7,6},{9,8},{10,9},{11,10},{12... | collective-permute-start | bytes 110600 | tf_op jit(solution)/shard_map/ppermute | solution.py:20
  47.8 32.1 %all-to-all-start.1 = ((f32[16,4,4096]{2,0,1:T(8,128)}), f32[16,4,4096]{2,0,1:T(8,128)}, u32[]{:S(2)}, u32[]{:S(2)}) async-start(f32[16,4,4096]{2,0,1:T(8,128)} %bitcast.97), calls=%async_computation.1 | async-start | bytes 2097152 | tf_op jit(solution)/shard_map/all_to_all | solution.py:142
  69.7 1.9 %copy-start.6 = (f32[64,512]{1,0:T(8,128)}, f32[64,512]{1,0:T(8,128)S(1)}, u32[]{:S(2)}) copy-start(f32[64,512]{1,0:T(8,128)S(1)} %all-gather) | copy-start | bytes 393220
  71.6 4.1 %copy-start = (f32[18,16384]{1,0:T(8,128)S(1)}, f32[18,16384]{1,0:T(8,128)}, u32[]{:S(2)}) copy-start(f32[18,16384]{1,0:T(8,128)} %get-tuple-element.90) | copy-start | bytes 3538948
  75.7 2.8 %copy-start.4 = (f32[18,4,512]{2,0,1:T(8,128)}, f32[18,4,512]{2,0,1:T(8,128)S(1)}, u32[]{:S(2)}) copy-start(f32[18,4,512]{2,0,1:T(8,128)S(1)} %copy.119) | copy-start | bytes 442372
  79.9 4.3 %copy-start.7 = (f32[64,512]{1,0:T(8,128)S(1)}, f32[64,512]{1,0:T(8,128)}, u32[]{:S(2)}) copy-start(f32[64,512]{1,0:T(8,128)} %copy-done.6) | copy-start | bytes 393220
  79.9 22.8 %copy-start.5 = (f32[18,4,512]{2,0,1:T(8,128)S(1)}, f32[18,4,512]{2,0,1:T(8,128)}, u32[]{:S(2)}) copy-start(f32[18,4,512]{2,0,1:T(8,128)} %copy-done.4) | copy-start | bytes 442372
  79.9 26.4 %all-to-all-start = ((f32[16,4,5120]{2,0,1:T(8,128)}), f32[16,4,5120]{2,0,1:T(8,128)S(1)}, u32[]{:S(2)}, u32[]{:S(2)}) async-start(f32[16,4,5120]{2,0,1:T(8,128)} %slice.254), calls=%async_computation | async-start | bytes 2621440 | tf_op jit(solution)/shard_map/all_to_all | solution.py:141
  107.2 1.2 copy-start.1
  109.3 1.7 copy-start.10
  115.7 2.0 %copy-start.8 = (f32[64,64]{1,0:T(8,128)S(1)}, f32[64,64]{1,0:T(8,128)}, u32[]{:S(2)}) copy-start(f32[64,64]{1,0:T(8,128)} %fusion.67) | copy-start | bytes 49156
where the time goes:
time: 182 us; the launch traced here: 181 us
  blocking collectives  58.6 us (32%)
  local copies, waits for them, and re-layouts  49.4 us (27%)
  matrix products  26.1 us (14%)
  starting transfers between devices  23.9 us (13%)
  other arithmetic  18 us (10%)
  between operations  3.7 us (2%)
    all_to_all x1, blocking collectives, shards(): lax.all_to_all(analysed.reshape(2, members, quart_cells), 'mem', split_ax...  29.7 us
    dot_general x37, matrix products, batch_product(): jnp.einsum('uij,ujk->uik', first, second, precision=lax.Precision.HIGHEST)  18.8 us
    psum x1, blocking collectives, shards(): lax.psum((jnp.sum(innov_seen * innov_seen), jnp.sum(scaled_seen * scaled_...  16.1 us
    all_gather x1, blocking collectives, shards(): seen_all = lax.all_gather(seen_local, 'mem', axis=0, tiled=True)  12.8 us
    ppermute x3, starting transfers between devices, padded_2(): lax.ppermute(lax.slice_in_dim(block, block.shape[dim] - width, None, axis...  11.9 us
    unnamed x37, local copies, waits for them, and re-layouts  8.82 us
    concatenate x2, local copies, waits for them, and re-layouts, padded_2(): block = jnp.concatenate([low, block, high], axis=dim)  6.12 us
    another operation x5, other arithmetic, shards(): padded = padded_2(jnp.stack([depth_now, flow_now]), (('cell', 2),), 1)  5.41 us
  transfers between devices with their start and end apart: 8, of which 0 were waited for; matrix products, arithmetic and copies ran while one was open for 20% of the time, Pallas kernels for 0%

commit v1 on v0

--- a/solution.py
+++ b/solution.py
@@ -122,7 +122,12 @@
     extended = padded_2(stacked, (("cell", 1),), PER)
     row_total = extended.shape[0]
     seen_local = depth_now[:, offsets]
-    seen_all = lax.all_gather(seen_local, "mem", axis=0, tiled=True)
+    ring = [seen_local]
+    for hop in range(3):
+        ring.append(lax.ppermute(ring[-1], "mem", [(dev, (dev + 1) % 4) for dev in range(4)]))
+    seen_all = jnp.roll(
+        jnp.concatenate(ring[::-1], axis=0), (lax.axis_index("mem") + 1) * ring[0].shape[0], axis=0
+    )
     seen_mean = jnp.mean(seen_all, axis=0)
     scaled_seen = (seen_all - seen_mean[None, :]) * precision_obs[None, :]
     innov_seen = (values_obs - seen_mean) * precision_obs

time: 182 us -> 200 us (1.099)
  waiting for transfers between devices: 0.02 us -> 22.5 us
  blocking collectives: 58.6 us -> 45.7 us
  local copies, waits for them, and re-layouts: 49.4 us -> 53.6 us
  starting transfers between devices: 23.9 us -> 26.9 us
    ppermute x0 -> x3, waiting for transfers between devices: none -> 21.1 us  [shards(): lax.ppermute(ring[-1], 'mem', [(dev, (dev + 1) % 4) for dev in range(4)])]
    all_gather x1 -> x0, blocking collectives: 12.8 us -> none  [shards(): seen_all = lax.all_gather(seen_local, 'mem', axis=0, tiled=True)]
    ppermute x0 -> x3, starting transfers between devices: none -> 4.08 us  [shards(): lax.ppermute(ring[-1], 'mem', [(dev, (dev + 1) % 4) for dev in range(4)])]
    gather x2 -> x1, local copies, waits for them, and re-layouts: 4.51 us -> 5.02 us  [shards(): seen_local = depth_now[:, offsets]]
    unnamed x37 -> x35, local copies, waits for them, and re-layouts: 8.82 us -> 8.56 us
  transfers between devices with their start and end apart: 8 -> 11, of which waited for: 0 -> 4; matrix products, arithmetic and copies ran while one was open for 20% -> 17% of each run, Pallas kernels for 0% -> 0%
where the time goes in v1:
time: 200 us; the launch traced here: 199 us
  local copies, waits for them, and re-layouts  53.6 us (27%)
  blocking collectives  45.7 us (23%)
  starting transfers between devices  26.9 us (13%)
  matrix products  26.1 us (13%)
  waiting for transfers between devices  22.5 us (11%)
  other arithmetic  19.8 us (10%)
  between operations  3.69 us (2%)
    all_to_all x1, blocking collectives, shards(): lax.all_to_all(analysed.reshape(2, members, quart_cells), 'mem', split_ax...  29.7 us
    ppermute x3, waiting for transfers between devices, shards(): lax.ppermute(ring[-1], 'mem', [(dev, (dev + 1) % 4) for dev in range(4)])  21.1 us
    dot_general x37, matrix products, batch_product(): jnp.einsum('uij,ujk->uik', first, second, precision=lax.Precision.HIGHEST)  18.8 us
    psum x1, blocking collectives, shards(): lax.psum((jnp.sum(innov_seen * innov_seen), jnp.sum(scaled_seen * scaled_...  15.9 us
    ppermute x3, starting transfers between devices, padded_2(): lax.ppermute(lax.slice_in_dim(block, block.shape[dim] - width, None, axis...  11.9 us
    unnamed x35, local copies, waits for them, and re-layouts  8.56 us
    div x2, other arithmetic, face_fluxes(): (fastest * moment_left - slowest * moment_right + slowest * fastest * (sa...  5.46 us
    concatenate x2, local copies, waits for them, and re-layouts, padded_2(): block = jnp.concatenate([low, block, high], axis=dim)  5.46 us
  transfers between devices with their start and end apart: 11, of which 4 were waited for; matrix products, arithmetic and copies ran while one was open for 17% of the time, Pallas kernels for 0%

profile of v1, /device:TPU:0, one launch (start us, length us, event | category | flops | bytes accessed | tf_op | source)
XLA Modules:
  0.0 199.3 jit_solution(14561258437893585830)
XLA Ops:
  3.7 3.0 %collective-permute-start = (f32[2,16,1]{2,1,0:T(8,128)S(1)}, f32[2,16,1]{2,1,0:T(8,128)S(1)}, u32[]{:S(2)}, u32[]{:S(2)}) collective-permute-start(f32[2,16,1]{2,1,0:T(8,128)S(1)} %get-tuple-element.88), channel_id=1, source_target_pairs={{0,1},{1,2},{2,3},{3,4},{4,5},{5,6},{6,7},{8,9},{9,10},{10,11},{11... | collective-permute-start | bytes 392 | tf_op jit(solution)/shard_map/ppermute | solution.py:17
  9.0 2.5 %scatter_custom_fusion.1 = f32[16384]{0:T(1024)S(1)} fusion(s32[512]{0:T(512)S(1)} %bitcast.155, f32[512]{0:T(512)S(1)} %bitcast.149, f32[]{:T(128)} %constant.90.clone.1), kind=kCustom, calls=%fused_computation.139 | custom fusion | bytes 65540 | tf_op jit(solution)/shard_map/scatter | solution.py:120
  11.5 2.6 %scatter_custom_fusion = f32[16384]{0:T(1024)S(1)} fusion(s32[512]{0:T(512)S(1)} %bitcast.156, f32[512]{0:T(512)} %bitcast.157, f32[]{:T(128)} %constant.90.clone.1), kind=kCustom, calls=%fused_computation.141 | custom fusion | bytes 66048 | tf_op jit(solution)/shard_map/scatter | solution.py:119
  15.6 3.1 %concatenate.40 = f32[2,16,16386]{2,1,0:T(8,128)S(1)} concatenate(f32[2,16,1]{2,1,0:T(8,128)S(1)} %collective-permute-done, f32[2,16,16384]{2,1,0:T(8,128)} %pad_maximum_fusion, f32[2,16,1]{2,1,0:T(8,128)S(1)} %collective-permute-done.1), dimensions={2} | concatenate | bytes 4194816 | tf_op jit(solution)/shard_map/concatenate | solution.py:21
  18.8 2.2 %fusion.12 = (f32[16,16385]{1,0:T(8,128)S(1)}, f32[16,16385]{1,0:T(8,128)S(1)}, f32[16,16385]{1,0:T(8,128)S(1)}, f32[16,16385]{1,0:T(8,128)S(1)}) fusion(f32[16,16386]{1,0:T(8,128)S(1)} %get-tuple-element.82, pred[16385]{0:T(1024)(128)(4,1)S(1)} %fusion.58, f32[16,16386]{1,0:T(8,128)S(1)} %get-tuple-element.81), kind=kLoop, calls=%fused_computation.43 | loop fusion | flops 10748560 | bytes 8405505 | tf_op jit(solution)/shard_map/div | solution.py:43
  23.8 5.2 %collective-permute-start.2 = (f32[2,16,1]{2,1,0:T(8,128)S(1)}, f32[2,16,1]{2,1,0:T(8,128)S(1)}, u32[]{:S(2)}, u32[]{:S(2)}) collective-permute-start(f32[2,16,1]{2,1,0:T(8,128)S(1)} %get-tuple-element.86), channel_id=1, source_target_pairs={{0,1},{1,2},{2,3},{3,4},{4,5},{5,6},{6,7},{8,9},{9,10},{10,11},{11... | collective-permute-start | bytes 392 | tf_op jit(solution)/shard_map/ppermute | solution.py:17
  29.8 2.4 %concatenate.42 = f32[2,16,16386]{2,1,0:T(8,128)} concatenate(f32[2,16,1]{2,1,0:T(8,128)S(1)} %collective-permute-done.2, f32[2,16,16384]{2,1,0:T(8,128)S(1)} %pad_maximum_fusion.1, f32[2,16,1]{2,1,0:T(8,128)S(1)} %collective-permute-done.3), dimensions={2} | concatenate | bytes 4194816 | tf_op jit(solution)/shard_map/concatenate | solution.py:21
  32.2 1.7 slice_bitcast_fusion.1
  33.9 3.3 %fusion.19 = (f32[16,16385]{1,0:T(8,128)S(1)}, f32[16,16385]{1,0:T(8,128)S(1)}, f32[16,16385]{1,0:T(8,128)}, f32[16,16385]{1,0:T(8,128)}) fusion(f32[16,16386]{1,0:T(8,128)S(1)} %get-tuple-element.80, pred[16385]{0:T(1024)(128)(4,1)S(1)} %fusion.58, f32[16,16386]{1,0:T(8,128)S(1)} %get-tuple-element.79), kind=kLoop, calls=%fused_computation.50 | loop fusion | flops 10748560 | bytes 8405505 | tf_op jit(solution)/shard_map/div | solution.py:43
  37.8 4.6 %copy.122 = f32[16,16384]{0,1:T(8,128)} copy(f32[16,16384]{1,0:T(8,128)S(1)} %fusion.35) | data formatting | bytes 2097152 | tf_op jit(solution)/shard_map/add | solution.py:56
  42.4 3.7 %collective-permute-start.4 = (f32[18,512]{1,0:T(8,128)S(1)}, f32[18,512]{1,0:T(8,128)S(1)}, u32[]{:S(2)}, u32[]{:S(2)}) collective-permute-start(f32[18,512]{1,0:T(8,128)S(1)} %get-tuple-element.91), channel_id=1, source_target_pairs={{0,1},{1,2},{2,3},{3,4},{4,5},{5,6},{6,7},{8,9},{9,10},{10,11},{11... | collective-permute-start | bytes 110600 | tf_op jit(solution)/shard_map/ppermute | solution.py:17
  47.4 5.0 %gather_fusion = f32[512,16]{1,0:T(8,128)} fusion(f32[16,16384]{0,1:T(8,128)} %copy.122, s32[1024]{0:T(1024)S(1)} %pad_clamp_fusion), kind=kCustom, calls=%fused_computation | custom fusion | bytes 67584 | tf_op jit(solution)/shard_map/gather | solution.py:124
  53.9 2.4 %fusion.31 = f32[16,16384]{1,0:T(8,128)S(1)} fusion(f32[16,16385]{1,0:T(8,128)S(1)} %get-tuple-element.75, f32[16,16385]{1,0:T(8,128)} %get-tuple-element.94, f32[16,16385]{1,0:T(8,128)} %get-tuple-element.93, f32[16,16386]{1,0:T(8,128)S(1)} %get-tuple-element.80, pred[16384]{0:T(1024)(128)(4,1)S(1)} %get-tuple-element.102, ...), kind=kLoop, calls=%fused_computation.80 | loop fusion | flops 2359296 | bytes 6324224 | tf_op jit(solution)/shard_map/sub | solution.py:57
  57.4 3.5 %all-to-all-start.1 = ((f32[16,4,4096]{2,0,1:T(8,128)}), f32[16,4,4096]{2,0,1:T(8,128)S(1)}, u32[]{:S(2)}, u32[]{:S(2)}) async-start(f32[16,4,4096]{2,0,1:T(8,128)} %bitcast.97), calls=%async_computation.1 | async-start | bytes 2097152 | tf_op jit(solution)/shard_map/all_to_all | solution.py:147
  61.0 2.0 %collective-permute-start.7 = (f32[16,512]{0,1:T(8,128)}, f32[16,512]{0,1:T(8,128)}, u32[]{:S(2)}, u32[]{:S(2)}) collective-permute-start(f32[16,512]{0,1:T(8,128)} %collective-permute-done.6), channel_id=1, source_target_pairs={{0,8},{8,16},{16,24},{24,0},{1,9},{9,17},{17,25},{25,1},{2,10},{10... | collective-permute-start | bytes 98312 | tf_op jit(solution)/shard_map/ppermute | solution.py:127
  63.0 1.8 pad_maximum_fusion.6
  64.9 3.0 %reshape.149 = f32[18,4,4096]{2,1,0:T(4,128)} reshape(f32[18,16384]{1,0:T(8,128)} %get-tuple-element.89) | data formatting | bytes 2359296 | tf_op jit(solution)/shard_map/reshape | solution.py:138
  68.9 3.0 %reshape.150 = f32[18,4,4096]{2,1,0:T(4,128)} reshape(f32[18,16384]{1,0:T(8,128)} %get-tuple-element.90) | data formatting | bytes 2359296 | tf_op jit(solution)/shard_map/reshape | solution.py:140
  75.9 3.5 %all-to-all-start = ((f32[16,4,5120]{2,0,1:T(8,128)}), f32[16,4,5120]{2,0,1:T(8,128)S(1)}, u32[]{:S(2)}, u32[]{:S(2)}) async-start(f32[16,4,5120]{2,0,1:T(8,128)} %slice.254), calls=%async_computation | async-start | bytes 2621440 | tf_op jit(solution)/shard_map/all_to_all | solution.py:146
  82.2 19.6 %collective-permute-done.8 = f32[16,512]{0,1:T(8,128)S(1)} collective-permute-done((f32[16,512]{0,1:T(8,128)}, f32[16,512]{0,1:T(8,128)S(1)}, u32[]{:S(2)}, u32[]{:S(2)}) %collective-permute-start.8) | collective-permute-done | bytes 32800 | tf_op jit(solution)/shard_map/ppermute | solution.py:127
  101.9 1.9 concatenate.51
  106.1 15.9 %all-reduce = (f32[]{:T(128)}, f32[]{:T(128)}) all-reduce(f32[]{:T(128)} %get-tuple-element.104, f32[]{:T(128)S(6)} %div.103), channel_id=1, replica_groups=mesh['mem'=4,'cell'=8] {'cell'}, use_global_device_ids=true, to_apply=%region_5.6 | all-reduce | flops 2 | bytes 16 | tf_op jit(solution)/shard_map/psum | solution.py:134
  127.9 1.7 squeeze.49
  129.6 1.9 subtract_multiply_fusion
  131.4 2.8 %fusion.43 = f32[10,64,64]{2,1,0:T(8,128)S(1)} fusion(f32[64,10,512]{2,1,0:T(8,128)S(1)} %subtract_multiply_fusion), kind=kOutput, calls=%fused_computation.98 | convolution fusion | flops 251658240 | bytes 1474560 | tf_op jit(solution)/shard_map/ibr,jbr->bij/dot_general | solution.py:158
  134.2 2.0 fusion.41
  136.7 19.9 %while.14 = (s32[]{:T(128)}, f32[8,64,64]{1,2,0:T(8,128)S(1)}, f32[8,64,64]{2,1,0:T(8,128)S(1)}, s32[]{:T(128)}) while((s32[]{:T(128)}, f32[8,64,64]{1,2,0:T(8,128)S(1)}, f32[8,64,64]{2,1,0:T(8,128)S(1)}, s32[]{:T(128)}) %tuple.56), condition=%wide.region_11.12_spmd.clone, body=%wide.region_10.11_spmd.clone.sunk | while | flops 75571200 | bytes 1736757 | solution.py:78
  157.5 2.1 %bitcast_add_fusion = f32[2,64,8,512]{3,1,0,2:T(8,128)S(1)} fusion(f32[2,64,8,512]{3,1,0,2:T(8,128)S(1)} %copy_dynamic-update-slice_fusion, f32[2,8,512]{2,0,1:T(2,128)S(1)} %broadcast_multiply_fusion, f32[8,64,64]{2,1,0:T(8,128)S(1)} %get-tuple-element.36, f32[8,64]{1,0:T(8,128)S(1)} %broadcast_multiply_fusion.2, f32[8]{0:T(128)S(1)} %get-tuple-element.105, ...), kind=kOutput, calls=%fused_computation.19 | convolution fusion | flops 403800064 | bytes 4360228 | tf_op jit(solution)/shard_map/fipr,pij->fjpr/dot_general | solution.py:169
  160.8 2.8 %reshape.182 = f32[2,64,4096]{2,0,1:T(2,128)} reshape(f32[2,64,8,512]{3,2,0,1:T(8,128)S(1)} %copy.142) | data formatting | bytes 4194304 | tf_op jit(solution)/shard_map/reshape | solution.py:173
  163.6 29.7 %all_to_all.45 = f32[2,64,4096]{2,0,1:T(2,128)S(1)} all-to-all(f32[2,64,4096]{2,0,1:T(2,128)} %reshape.182), channel_id=1, replica_groups=mesh['mem'=4,'cell'=8] {'mem'}, dimensions={1} | all-to-all | bytes 4194304 | tf_op jit(solution)/shard_map/all_to_all | solution.py:172
  195.4 1.6 copy.149
  197.7 1.6 copy.148
  (175 shorter events, 52.5 us)
Async XLA Ops:
  1.5 5.9 %copy-start.3 = (f32[16,16384]{1,0:T(8,128)S(1)}, f32[16,16384]{1,0:T(8,128)}, u32[]{:S(2)}) copy-start(f32[16,16384]{1,0:T(8,128)} %param.12) | copy-start | bytes 3145732
  1.5 5.9 %copy-start.4 = (f32[16,16384]{1,0:T(8,128)S(1)}, f32[16,16384]{1,0:T(8,128)}, u32[]{:S(2)}) copy-start(f32[16,16384]{1,0:T(8,128)} %param.13) | copy-start | bytes 3145732
  2.5 13.1 %collective-permute-start.1 = (f32[2,16,1]{2,1,0:T(8,128)S(1)}, f32[2,16,1]{2,1,0:T(8,128)S(1)}, u32[]{:S(2)}, u32[]{:S(2)}) collective-permute-start(f32[2,16,1]{2,1,0:T(8,128)S(1)} %get-tuple-element.87), channel_id=1, source_target_pairs={{1,0},{2,1},{3,2},{4,3},{5,4},{6,5},{7,6},{9,8},{10,9},{11,10},{12... | collective-permute-start | bytes 392 | tf_op jit(solution)/shard_map/ppermute | solution.py:20
  3.7 11.8 %collective-permute-start = (f32[2,16,1]{2,1,0:T(8,128)S(1)}, f32[2,16,1]{2,1,0:T(8,128)S(1)}, u32[]{:S(2)}, u32[]{:S(2)}) collective-permute-start(f32[2,16,1]{2,1,0:T(8,128)S(1)} %get-tuple-element.88), channel_id=1, source_target_pairs={{0,1},{1,2},{2,3},{3,4},{4,5},{5,6},{6,7},{8,9},{9,10},{10,11},{11... | collective-permute-start | bytes 392 | tf_op jit(solution)/shard_map/ppermute | solution.py:17
  7.4 1.5 copy-start.12
  7.4 1.5 copy-start.13
  7.4 8.0 %copy-start.6 = (s32[2,16384]{1,0:T(2,128)S(1)}, s32[2,16384]{1,0:T(2,128)}, u32[]{:S(2)}) copy-start(s32[2,16384]{1,0:T(2,128)} %param.15) | copy-start | bytes 393220
  7.4 8.1 %copy-start.8 = (f32[16384]{0:T(1024)S(1)}, f32[16384]{0:T(1024)}, u32[]{:S(2)}) copy-start(f32[16384]{0:T(1024)} %param.16) | copy-start | bytes 196612
  8.9 6.6 %copy-start.9 = (f32[1,512]{1,0:T(1,128)}, f32[1,512]{1,0:T(1,128)S(1)}, u32[]{:S(2)}) copy-start(f32[1,512]{1,0:T(1,128)S(1)} %broadcast_divide_fusion.1) | copy-start | bytes 6148
  22.5 6.7 %collective-permute-start.3 = (f32[2,16,1]{2,1,0:T(8,128)S(1)}, f32[2,16,1]{2,1,0:T(8,128)S(1)}, u32[]{:S(2)}, u32[]{:S(2)}) collective-permute-start(f32[2,16,1]{2,1,0:T(8,128)S(1)} %get-tuple-element.85), channel_id=1, source_target_pairs={{1,0},{2,1},{3,2},{4,3},{5,4},{6,5},{7,6},{9,8},{10,9},{11,10},{12... | collective-permute-start | bytes 392 | tf_op jit(solution)/shard_map/ppermute | solution.py:20
  23.8 6.0 %collective-permute-start.2 = (f32[2,16,1]{2,1,0:T(8,128)S(1)}, f32[2,16,1]{2,1,0:T(8,128)S(1)}, u32[]{:S(2)}, u32[]{:S(2)}) collective-permute-start(f32[2,16,1]{2,1,0:T(8,128)S(1)} %get-tuple-element.86), channel_id=1, source_target_pairs={{0,1},{1,2},{2,3},{3,4},{4,5},{5,6},{6,7},{8,9},{9,10},{10,11},{11... | collective-permute-start | bytes 392 | tf_op jit(solution)/shard_map/ppermute | solution.py:17
  42.4 20.6 %collective-permute-start.4 = (f32[18,512]{1,0:T(8,128)S(1)}, f32[18,512]{1,0:T(8,128)S(1)}, u32[]{:S(2)}, u32[]{:S(2)}) collective-permute-start(f32[18,512]{1,0:T(8,128)S(1)} %get-tuple-element.91), channel_id=1, source_target_pairs={{0,1},{1,2},{2,3},{3,4},{4,5},{5,6},{6,7},{8,9},{9,10},{10,11},{11... | collective-permute-start | bytes 110600 | tf_op jit(solution)/shard_map/ppermute | solution.py:17
  46.1 16.9 %collective-permute-start.5 = (f32[18,512]{1,0:T(8,128)S(1)}, f32[18,512]{1,0:T(8,128)S(1)}, u32[]{:S(2)}, u32[]{:S(2)}) collective-permute-start(f32[18,512]{1,0:T(8,128)S(1)} %get-tuple-element.92), channel_id=1, source_target_pairs={{1,0},{2,1},{3,2},{4,3},{5,4},{6,5},{7,6},{9,8},{10,9},{11,10},{12... | collective-permute-start | bytes 110600 | tf_op jit(solution)/shard_map/ppermute | solution.py:20
  52.4 8.6 %collective-permute-start.6 = (f32[16,512]{0,1:T(8,128)}, f32[16,512]{0,1:T(8,128)}, u32[]{:S(2)}, u32[]{:S(2)}) collective-permute-start(f32[16,512]{0,1:T(8,128)} %bitcast.141), channel_id=1, source_target_pairs={{0,8},{8,16},{16,24},{24,0},{1,9},{9,17},{17,25},{25,1},{2,10},{10... | collective-permute-start | bytes 98312 | tf_op jit(solution)/shard_map/ppermute | solution.py:127
  57.4 17.5 %all-to-all-start.1 = ((f32[16,4,4096]{2,0,1:T(8,128)}), f32[16,4,4096]{2,0,1:T(8,128)S(1)}, u32[]{:S(2)}, u32[]{:S(2)}) async-start(f32[16,4,4096]{2,0,1:T(8,128)} %bitcast.97), calls=%async_computation.1 | async-start | bytes 2097152 | tf_op jit(solution)/shard_map/all_to_all | solution.py:147
  61.0 19.9 %collective-permute-start.7 = (f32[16,512]{0,1:T(8,128)}, f32[16,512]{0,1:T(8,128)}, u32[]{:S(2)}, u32[]{:S(2)}) collective-permute-start(f32[16,512]{0,1:T(8,128)} %collective-permute-done.6), channel_id=1, source_target_pairs={{0,8},{8,16},{16,24},{24,0},{1,9},{9,17},{17,25},{25,1},{2,10},{10... | collective-permute-start | bytes 98312 | tf_op jit(solution)/shard_map/ppermute | solution.py:127
  74.9 1.0 copy-start
  75.9 49.0 %all-to-all-start = ((f32[16,4,5120]{2,0,1:T(8,128)}), f32[16,4,5120]{2,0,1:T(8,128)S(1)}, u32[]{:S(2)}, u32[]{:S(2)}) async-start(f32[16,4,5120]{2,0,1:T(8,128)} %slice.254), calls=%async_computation | async-start | bytes 2621440 | tf_op jit(solution)/shard_map/all_to_all | solution.py:146
  80.9 20.9 %collective-permute-start.8 = (f32[16,512]{0,1:T(8,128)}, f32[16,512]{0,1:T(8,128)S(1)}, u32[]{:S(2)}, u32[]{:S(2)}) collective-permute-start(f32[16,512]{0,1:T(8,128)} %collective-permute-done.7), channel_id=1, source_target_pairs={{0,8},{8,16},{16,24},{24,0},{1,9},{9,17},{17,25},{25,1},{2,10},{10... | collective-permute-start | bytes 98312 | tf_op jit(solution)/shard_map/ppermute | solution.py:127
  82.2 21.9 %copy-start.10 = (f32[1,512]{1,0:T(1,128)S(1)}, f32[1,512]{1,0:T(1,128)}, u32[]{:S(2)}) copy-start(f32[1,512]{1,0:T(1,128)} %copy-done.9) | copy-start | bytes 6148
  82.2 21.9 %copy-start.11 = (f32[1,512]{1,0:T(1,128)S(1)}, f32[1,512]{1,0:T(1,128)}, u32[]{:S(2)}) copy-start(f32[1,512]{1,0:T(1,128)} %param.18) | copy-start | bytes 6148
  82.2 41.1 %copy-start.1 = (f32[16,4,4096]{2,0,1:T(8,128)S(1)}, f32[16,4,4096]{2,0,1:T(8,128)}, u32[]{:S(2)}) copy-start(f32[16,4,4096]{2,0,1:T(8,128)} %copy-done) | copy-start | bytes 3145732
  125.7 1.2 copy-start.2
  127.9 1.7 copy-start.7
  134.2 2.0 copy-start.5
